TPU v7x, 32 devices: a whole 2x2x4 slice. The times are simulated.
32 devices in a mesh: dp: 4 (over y, core), fsdp: 8 (over z, x).
Axes of the slice: x: 2, y: 2, z: 4, core: 2. Of those that a mesh axis runs over, the one named last changes fastest.
Arguments:
- hidden_in: bfloat16 [20480, 768], P(('dp', 'fsdp')), may hold values from -7 to 7
- prev_logits: bfloat16 [32, 12, 640, 640], P(('dp', 'fsdp')), may hold values from -6 to 6
- segment_ids: int32 [32, 640], P(('dp', 'fsdp')), may hold values from 0 to 3, never falling along the last dimension, each value on 1 to 320 neighbouring positions
- d_hidden: bfloat16 [20480, 768], P(('dp', 'fsdp')), may hold values from -6 to 6
- d_logits: bfloat16 [32, 12, 640, 640], P(('dp', 'fsdp')), may hold values from -3 to 3
- weight_in: float32 [768, 5376], P(('dp', 'fsdp')), may hold values from -2.5 to 2.5
- weight_out: float32 [3840, 768], P(('dp', 'fsdp')), may hold values from -2 to 2
- vectors: float32 [12, 768], P(None, ('dp', 'fsdp')), may hold values from -0.6 to 1.45
- moment_in: float32 [768, 5376], P(('dp', 'fsdp')), may hold values from -0.55 to 0.55
- moment_out: float32 [3840, 768], P(('dp', 'fsdp')), may hold values from -0.55 to 0.55
- moment_vectors: float32 [12, 768], P(None, ('dp', 'fsdp')), may hold values from -1.5 to 1.5
- square_in: float32 [768, 5376], P(('dp', 'fsdp')), may hold values from 0.001 to 0.004
- square_out: float32 [3840, 768], P(('dp', 'fsdp')), may hold values from 0.001 to 0.004
- square_vectors: float32 [12, 768], P(None, ('dp', 'fsdp')), may hold values from 0.008 to 0.032
- step_count: int32 [1], replicated, may hold values from 1 to 20
Outputs:
- hidden_out: bfloat16 [20480, 768], P(('dp', 'fsdp'))
- logits: bfloat16 [32, 12, 640, 640], P(('dp', 'fsdp'))
- d_input: bfloat16 [20480, 768], P(('dp', 'fsdp'))
- d_prev: bfloat16 [32, 12, 640, 640], P(('dp', 'fsdp'))
- grad_weight_in: float32 [768, 5376], P(('dp', 'fsdp'))
- grad_weight_out: float32 [3840, 768], P(('dp', 'fsdp'))
- grad_vectors: float32 [12, 768], P(None, ('dp', 'fsdp'))
- new_moment_in: float32 [768, 5376], P(('dp', 'fsdp'))
- new_moment_out: float32 [3840, 768], P(('dp', 'fsdp'))
- new_moment_vectors: float32 [12, 768], P(None, ('dp', 'fsdp'))
- new_square_in: float32 [768, 5376], P(('dp', 'fsdp'))
- new_square_out: float32 [3840, 768], P(('dp', 'fsdp'))
- new_square_vectors: float32 [12, 768], P(None, ('dp', 'fsdp'))
- new_weight_in: float32 [768, 5376], P(('dp', 'fsdp'))
- new_weight_out: float32 [3840, 768], P(('dp', 'fsdp'))
- new_vectors: float32 [12, 768], P(None, ('dp', 'fsdp'))
- copy_weight_in: bfloat16 [768, 5376], P(('dp', 'fsdp'))
- copy_weight_out: bfloat16 [3840, 768], P(('dp', 'fsdp'))
- copy_vectors: bfloat16 [12, 768], P(None, ('dp', 'fsdp'))
- grad_norm: float32 [], replicated
Inputs may be any that keep to these rules, and one draw needn't show every extreme that they name: `segment_ids`: along each row the segment numbers never fall; no segment holds more than 320 slots.
All inputs are finite; a program needn't handle non-finite values.
Results may differ from a plain program's by a relative error of at most 0.012.
Values may be sent and summed in bfloat16 or wider, within the bound.
A program may use at most 192 MiB of HBM per device.

v0:
```python
import math
import jax
import jax.numpy as jnp
from jax import lax
from jax.sharding import PartitionSpec as P

PARAMS = 7087104
norm_eps = 1e-12
clip_scale = 1.0
beta_one = 0.9
beta_two = 0.999
adam_eps = 1e-08
rate_matrix = 0.06
rate_vector = 0.25
decay_matrix = 0.01
masked_fill = -1e30


def gelu_exact(upward):
    return jax.nn.gelu(upward, approximate=False)


def norm_rows(residual, gain_row, shift_row):
    centered = residual - jnp.mean(residual, axis=1, keepdims=True)
    scaling = lax.rsqrt(jnp.mean(centered * centered, axis=1, keepdims=True) + norm_eps)
    normed = centered * scaling
    return (normed * gain_row + shift_row, normed, scaling)


def norm_back(grad_after, normed, scaling, gain_row):
    scaled_grad = grad_after * gain_row
    return scaling * (
        scaled_grad
        - jnp.mean(scaled_grad, axis=1, keepdims=True)
        - normed * jnp.mean(scaled_grad * normed, axis=1, keepdims=True)
    )


def split_heads(matrix, head_count):
    return matrix.reshape(matrix.shape[0], head_count, -1)


def forward(weights, tokens, previous, same_doc):
    weight_in, weight_out, vectors = weights
    model_width = weight_out.shape[1]
    head_count = previous.shape[0]
    row_count = tokens.shape[0]
    score_scale = (model_width // head_count) ** (-0.5)
    vector_rows = vectors.astype(jnp.float32)
    projected = jnp.dot(tokens, weight_in[:, : 3 * model_width], preferred_element_type=jnp.float32)
    queries = (projected[:, :model_width] + vector_rows[4]).astype(jnp.bfloat16)
    keys_low = projected[:, model_width : 2 * model_width].astype(jnp.bfloat16)
    values_low = (projected[:, 2 * model_width :] + vector_rows[5]).astype(jnp.bfloat16)
    scores = jnp.einsum(
        "qhd,khd->hqk",
        split_heads(queries, head_count),
        split_heads(keys_low, head_count),
        preferred_element_type=jnp.float32,
    ) * score_scale + previous.astype(jnp.float32)
    masked = jnp.where(same_doc[None], scores, masked_fill)
    row_max = jnp.max(masked, axis=2, keepdims=True)
    expo_terms = jnp.exp(masked - row_max)
    totals = jnp.sum(expo_terms, axis=2, keepdims=True)
    attn_probs = expo_terms / totals
    log_sums = row_max + jnp.log(totals)
    mixed_heads = jnp.einsum(
        "hqk,khd->qhd",
        attn_probs.astype(jnp.bfloat16),
        split_heads(values_low, head_count),
        preferred_element_type=jnp.float32,
    )
    mixed_heads = mixed_heads.reshape(row_count, model_width).astype(jnp.bfloat16)
    first_sum = tokens.astype(jnp.float32) + (
        jnp.dot(mixed_heads, weight_out[:model_width], preferred_element_type=jnp.float32)
        + vector_rows[6]
    )
    hidden_one, normed_one, scale_one = norm_rows(first_sum, vector_rows[0], vector_rows[2])
    hidden_low = hidden_one.astype(jnp.bfloat16)
    upward = jnp.dot(
        hidden_low, weight_in[:, 3 * model_width :], preferred_element_type=jnp.float32
    ) + vector_rows[8:].reshape(-1)
    activated = gelu_exact(upward).astype(jnp.bfloat16)
    second_sum = hidden_one + (
        jnp.dot(activated, weight_out[model_width:], preferred_element_type=jnp.float32)
        + vector_rows[7]
    )
    output, normed_two, scale_two = norm_rows(second_sum, vector_rows[1], vector_rows[3])
    kept_values = (
        queries,
        keys_low,
        values_low,
        log_sums,
        mixed_heads,
        normed_one,
        scale_one,
        hidden_low,
        upward,
        activated,
        normed_two,
        scale_two,
    )
    return (output, scores, kept_values)


def backward(weights, kept_values, tokens, previous, same_doc, grad_hidden, grad_logits):
    weight_in, weight_out, vectors = weights
    (
        queries,
        keys_low,
        values_low,
        log_sums,
        mixed_heads,
        normed_one,
        scale_one,
        hidden_low,
        upward,
        activated,
        normed_two,
        scale_two,
    ) = kept_values
    model_width = weight_out.shape[1]
    head_count = previous.shape[0]
    row_count = tokens.shape[0]
    score_scale = (model_width // head_count) ** (-0.5)
    vector_rows = vectors.astype(jnp.float32)
    grad_output = grad_hidden.astype(jnp.float32)
    gain_two_grad = jnp.sum(grad_output * normed_two, axis=0)
    shift_two_grad = jnp.sum(grad_output, axis=0)
    grad_second = norm_back(grad_output, normed_two, scale_two, vector_rows[1])
    grad_down = grad_second.astype(jnp.bfloat16)
    bias_down_grad = jnp.sum(grad_down, axis=0, dtype=jnp.float32)
    down_grad = jnp.einsum("tf,td->fd", activated, grad_down, preferred_element_type=jnp.float32)
    grad_activated = jnp.einsum(
        "td,fd->tf", grad_down, weight_out[model_width:], preferred_element_type=jnp.float32
    )
    unused_value, gelu_pull = jax.vjp(gelu_exact, upward)
    grad_up = gelu_pull(grad_activated)[0].astype(jnp.bfloat16)
    bias_up_grad = jnp.sum(grad_up, axis=0, dtype=jnp.float32)
    up_grad = jnp.einsum("td,tf->df", hidden_low, grad_up, preferred_element_type=jnp.float32)
    grad_hidden_one = grad_second + jnp.einsum(
        "tf,df->td", grad_up, weight_in[:, 3 * model_width :], preferred_element_type=jnp.float32
    )
    gain_one_grad = jnp.sum(grad_hidden_one * normed_one, axis=0)
    shift_one_grad = jnp.sum(grad_hidden_one, axis=0)
    grad_first = norm_back(grad_hidden_one, normed_one, scale_one, vector_rows[0])
    grad_attn = grad_first.astype(jnp.bfloat16)
    bias_out_grad = jnp.sum(grad_attn, axis=0, dtype=jnp.float32)
    attn_grad = jnp.einsum("tc,td->cd", mixed_heads, grad_attn, preferred_element_type=jnp.float32)
    grad_mixed = jnp.einsum(
        "td,cd->tc", grad_attn, weight_out[:model_width], preferred_element_type=jnp.float32
    ).astype(jnp.bfloat16)
    head_queries = split_heads(queries, head_count)
    head_keys = split_heads(keys_low, head_count)
    head_values = split_heads(values_low, head_count)
    head_grad_mixed = split_heads(grad_mixed, head_count)
    scores = jnp.einsum(
        "qhd,khd->hqk", head_queries, head_keys, preferred_element_type=jnp.float32
    ) * score_scale + previous.astype(jnp.float32)
    attn_probs = jnp.exp(jnp.where(same_doc[None], scores, masked_fill) - log_sums)
    grad_probs = jnp.einsum(
        "qhd,khd->hqk", head_grad_mixed, head_values, preferred_element_type=jnp.float32
    )
    grad_scores = attn_probs * (
        grad_probs - jnp.sum(attn_probs * grad_probs, axis=2, keepdims=True)
    )
    grad_total = (grad_scores + grad_logits.astype(jnp.float32)).astype(jnp.bfloat16)
    grad_queries = (
        (
            jnp.einsum("hqk,khd->qhd", grad_total, head_keys, preferred_element_type=jnp.float32)
            * score_scale
        )
        .astype(jnp.bfloat16)
        .reshape(row_count, model_width)
    )
    grad_keys = (
        (
            jnp.einsum("hqk,qhd->khd", grad_total, head_queries, preferred_element_type=jnp.float32)
            * score_scale
        )
        .astype(jnp.bfloat16)
        .reshape(row_count, model_width)
    )
    grad_values = (
        jnp.einsum(
            "hqk,qhd->khd",
            attn_probs.astype(jnp.bfloat16),
            head_grad_mixed,
            preferred_element_type=jnp.float32,
        )
        .astype(jnp.bfloat16)
        .reshape(row_count, model_width)
    )
    grad_projected = jnp.concatenate([grad_queries, grad_keys, grad_values], axis=1)
    qkv_grad = jnp.einsum("td,tc->dc", tokens, grad_projected, preferred_element_type=jnp.float32)
    grad_tokens = grad_first + jnp.einsum(
        "tc,dc->td",
        grad_projected,
        weight_in[:, : 3 * model_width],
        preferred_element_type=jnp.float32,
    )
    small_rows = jnp.stack(
        [
            gain_one_grad,
            gain_two_grad,
            shift_one_grad,
            shift_two_grad,
            jnp.sum(grad_queries, axis=0, dtype=jnp.float32),
            jnp.sum(grad_values, axis=0, dtype=jnp.float32),
            bias_out_grad,
            bias_down_grad,
        ]
    )
    small_grads = jnp.concatenate([small_rows, bias_up_grad.reshape(-1, model_width)], axis=0)
    return (
        jnp.concatenate([qkv_grad, up_grad], axis=1),
        jnp.concatenate([attn_grad, down_grad], axis=0),
        small_grads,
        grad_tokens.astype(jnp.bfloat16),
        grad_total,
    )


def adam_update(master, moment, square, gradient, factor, step_value, step_rate, decay_rate):
    clipped = gradient * factor
    new_moment = beta_one * moment + (1.0 - beta_one) * clipped
    new_square = beta_two * square + (1.0 - beta_two) * clipped * clipped
    fixed_moment = new_moment / (1.0 - jnp.power(beta_one, step_value))
    fixed_square = new_square / (1.0 - jnp.power(beta_two, step_value))
    updated = master - step_rate * (
        fixed_moment / (jnp.sqrt(fixed_square) + adam_eps) + decay_rate * master
    )
    return (clipped, new_moment, new_square, updated)


def body(
    hidden_in,
    prev_logits,
    segment_ids,
    d_hidden,
    d_logits,
    weight_in,
    weight_out,
    vectors,
    moment_in,
    moment_out,
    moment_vectors,
    square_in,
    square_out,
    square_vectors,
    step_count,
):
    low_in = weight_in.astype(jnp.bfloat16)
    low_out = weight_out.astype(jnp.bfloat16)
    low_small = vectors.astype(jnp.bfloat16)
    gathered = (
        lax.all_gather(low_in, ("dp", "fsdp"), axis=0, tiled=True),
        lax.all_gather(low_out, ("dp", "fsdp"), axis=0, tiled=True),
        lax.all_gather(low_small, ("dp", "fsdp"), axis=1, tiled=True),
    )
    segments = segment_ids[0]
    same_doc = segments[:, None] == segments[None, :]
    previous = prev_logits[0]
    output, scores, kept_values = forward(gathered, hidden_in, previous, same_doc)
    regathered = (
        lax.all_gather(low_in, ("dp", "fsdp"), axis=0, tiled=True),
        lax.all_gather(low_out, ("dp", "fsdp"), axis=0, tiled=True),
        lax.all_gather(low_small, ("dp", "fsdp"), axis=1, tiled=True),
    )
    unused_out, unused_scores, again_values = forward(regathered, hidden_in, previous, same_doc)
    full_in, full_out, full_small, grad_tokens, grad_prev = backward(
        regathered, again_values, hidden_in, previous, same_doc, d_hidden, d_logits[0]
    )
    owned_in, owned_out, owned_small = (
        lax.psum_scatter(full_in, ("dp", "fsdp"), scatter_dimension=0, tiled=True),
        lax.psum_scatter(full_out, ("dp", "fsdp"), scatter_dimension=0, tiled=True),
        lax.psum_scatter(full_small, ("dp", "fsdp"), scatter_dimension=1, tiled=True),
    )
    local_squares = (
        jnp.sum(owned_in * owned_in)
        + jnp.sum(owned_out * owned_out)
        + jnp.sum(owned_small * owned_small)
    )
    total_squares = lax.psum(local_squares, ("dp", "fsdp"))
    grad_norm = jnp.sqrt(total_squares)
    threshold = clip_scale * math.sqrt(PARAMS)
    factor = jnp.minimum(1.0, threshold / (grad_norm + 1e-06))
    step_value = step_count[0].astype(jnp.float32)
    clip_in, moment_one, square_one, updated_in = adam_update(
        weight_in, moment_in, square_in, owned_in, factor, step_value, rate_matrix, decay_matrix
    )
    clip_out, moment_two, square_two, updated_out = adam_update(
        weight_out, moment_out, square_out, owned_out, factor, step_value, rate_matrix, decay_matrix
    )
    clip_small, moment_three, square_three, updated_small = adam_update(
        vectors, moment_vectors, square_vectors, owned_small, factor, step_value, rate_vector, 0.0
    )
    return (
        output.astype(jnp.bfloat16),
        scores.astype(jnp.bfloat16)[None],
        grad_tokens,
        grad_prev[None],
        clip_in,
        clip_out,
        clip_small,
        moment_one,
        moment_two,
        moment_three,
        square_one,
        square_two,
        square_three,
        updated_in,
        updated_out,
        updated_small,
        updated_in.astype(jnp.bfloat16),
        updated_out.astype(jnp.bfloat16),
        updated_small.astype(jnp.bfloat16),
        grad_norm,
    )


def solution(mesh):
    return jax.shard_map(
        body,
        mesh=mesh,
        in_specs=(
            P(("dp", "fsdp"), None),
            P(("dp", "fsdp"), None, None, None),
            P(("dp", "fsdp"), None),
            P(("dp", "fsdp"), None),
            P(("dp", "fsdp"), None, None, None),
            P(("dp", "fsdp"), None),
            P(("dp", "fsdp"), None),
            P(None, ("dp", "fsdp")),
            P(("dp", "fsdp"), None),
            P(("dp", "fsdp"), None),
            P(None, ("dp", "fsdp")),
            P(("dp", "fsdp"), None),
            P(("dp", "fsdp"), None),
            P(None, ("dp", "fsdp")),
            P(),
        ),
        out_specs=(
            P(("dp", "fsdp"), None),
            P(("dp", "fsdp"), None, None, None),
            P(("dp", "fsdp"), None),
            P(("dp", "fsdp"), None, None, None),
            P(("dp", "fsdp"), None),
            P(("dp", "fsdp"), None),
            P(None, ("dp", "fsdp")),
            P(("dp", "fsdp"), None),
            P(("dp", "fsdp"), None),
            P(None, ("dp", "fsdp")),
            P(("dp", "fsdp"), None),
            P(("dp", "fsdp"), None),
            P(None, ("dp", "fsdp")),
            P(("dp", "fsdp"), None),
            P(("dp", "fsdp"), None),
            P(None, ("dp", "fsdp")),
            P(("dp", "fsdp"), None),
            P(("dp", "fsdp"), None),
            P(None, ("dp", "fsdp")),
            P(),
        ),
        check_vma=False,
    )
```

profile of v0, /device:TPU:0, one launch (start us, length us, event | category | flops | bytes accessed | tf_op | source)
XLA Modules:
  0.0 645.5 jit_solution(6729992086085996024)
XLA Ops:
  7.2 1.8 convert_element_type.143
  9.1 1.7 convert_element_type.154
  10.8 0.7 convert_bitcast_fusion.1
  11.5 71.6 %all-gather = bf16[32,24,12]{1,2,0:T(8,128)(2,1)S(1)} all-gather(bf16[1,24,12]{1,2,0:T(8,128)(2,1)S(1)} %convert_bitcast_fusion.1), channel_id=1, replica_groups=mesh['dp'=4,'fsdp'=8] {'dp','fsdp'}, dimensions={0}, use_global_device_ids=true | all-gather | bytes 19008 | tf_op jit(solution)/shard_map/all_gather | solution.py:258
  83.5 14.0 %copy.85 = bf16[1,12,640,640]{2,3,1,0:T(8,128)(2,1)} copy(bf16[1,12,640,640]{3,2,1,0:T(8,128)(2,1)} %param.16) | data formatting | bytes 19660800 | tf_op args[1]
  98.0 4.5 fusion.34
  102.6 1.3 fusion.45
  105.2 1.9 copy.82
  107.1 11.9 %select_reduce_fusion = (f32[12,640]{1,0:T(8,128)S(1)}, f32[12,640,640]{1,2,0:T(8,128)}) fusion(pred[640,640]{0,1:T(8,128)(4,1)S(1)} %broadcast_compare_fusion, bf16[1,12,640,640]{2,3,1,0:T(8,128)(2,1)} %copy.85, bf16[640,12,64]{0,2,1:T(8,128)(2,1)S(1)} %bitcast.63, bf16[640,12,64]{0,2,1:T(8,128)(2,1)S(1)} %bitcast.61), kind=kOutput, calls=%fused_computation.11 | convolution fusion | flops 653713920 | bytes 31897600 | tf_op jit(solution)/shard_map/qhd,khd->hqk/dot_general | solution.py:54
  119.0 17.7 %convert_bitcast_fusion = (bf16[1,12,640,640]{2,3,1,0:T(8,128)(2,1)}, f32[12,640]{1,0:T(8,128)S(1)}) fusion(f32[12,640,640]{1,2,0:T(8,128)} %get-tuple-element.143, f32[12,640]{1,0:T(8,128)S(1)} %get-tuple-element.142, pred[640,640]{0,1:T(8,128)(4,1)S(1)} %broadcast_compare_fusion), kind=kLoop, calls=%fused_computation.18 | loop fusion | flops 19653120 | bytes 29962240 | tf_op jit(solution)/shard_map/broadcast_in_dim | solution.py:299
  136.8 10.8 %fusion.55 = bf16[12,64,640]{2,1,0:T(8,128)(2,1)} fusion(bf16[640,12,64]{0,2,1:T(8,128)(2,1)S(1)} %bitcast.67, f32[12,640,640]{1,2,0:T(8,128)} %get-tuple-element.143, f32[12,640]{1,0:T(8,128)S(1)} %get-tuple-element.138, f32[12,640]{1,0:T(8,128)S(1)} %get-tuple-element.142, pred[640,640]{0,1:T(8,128)(4,1)S(1)} %broadcast_compare_fusion), kind=kOutput, calls=%fused_computation.92 | convolution fusion | flops 649297920 | bytes 22097920 | tf_op jit(solution)/shard_map/hqk,khd->qhd/dot_general | solution.py:66
  147.6 14.3 %all-gather.6.cloned.1.call-done = bf16[3840,768]{1,0:T(8,128)(2,1)} async-done(((bf16[120,768]{1,0:T(8,128)(2,1)}), bf16[3840,768]{1,0:T(8,128)(2,1)}) %all-gather.6.cloned.1.call-update) | async-done | bytes 5898256 | tf_op jit(solution)/shard_map/all_gather | solution.py:257
  161.9 3.1 fusion.86
  165.4 23.9 %multiply_convert_fusion = (bf16[640,3072]{1,0:T(8,128)(2,1)S(1)}, f32[640,3072]{1,0:T(8,128)}, f32[640,3072]{1,0:T(8,128)}) fusion(f32[3072]{0:T(1024)S(1)} %add.219, bf16[768,5376]{1,0:T(8,128)(2,1)} %all-gather.4.cloned.1.call-done, f32[640,768]{1,0:T(8,128)S(1)} %get-tuple-element.145, f32[768]{0:T(1024)S(1)} %get-tuple-element.111, ...), kind=kOutput, calls=%fused_computation.27 | convolution fusion | flops 3152117760 | bytes 26369024 | tf_op jit(solution)/shard_map/dot_general | solution.py:79
  189.3 3.4 fusion.87
  193.2 1.0 fusion.44
  194.2 1.8 convert_reduce_fusion.2
  195.9 6.4 fusion.69
  202.3 10.9 %convert_reduce_fusion = (f32[3072]{0:T(1024)S(1)}, bf16[640,3072]{1,0:T(8,128)(2,1)S(1)}) fusion(f32[640,3072]{1,0:T(8,128)} %get-tuple-element.136, bf16[3840,768]{1,0:T(8,128)(2,1)} %all-gather.6.cloned.1.call-done, f32[640,768]{1,0:T(8,128)S(1)} %get-tuple-element.132, f32[640,3072]{1,0:T(8,128)} %get-tuple-element.146, f32[3072]{0:T(1024)S(1)} %add.219), kind=kOutput, calls=%fused_computation.25 | convolution fusion | flops 3053810688 | bytes 26370048 | tf_op jit(solution)/shard_map/td,fd->tf/dot_general | solution.py:133
  213.3 3.8 multiply_reduce_fusion.1
  217.7 1.3 copy-done.6
  219.0 2.5 fusion.66
  221.5 9.5 %pad_maximum_fusion.1 = f32[3840,768]{1,0:T(8,128)} fusion(f32[3072,768]{1,0:T(8,128)} %fusion.69, f32[768,768]{1,0:T(8,128)} %fusion.66), kind=kLoop, calls=%fused_computation.13 | loop fusion | flops 2949120 | bytes 23592960 | tf_op jit(solution)/shard_map/concatenate | solution.py:216
  231.1 15.4 %copy.88 = bf16[1,12,640,640]{2,3,1,0:T(8,128)(2,1)} copy(bf16[1,12,640,640]{3,2,1,0:T(8,128)(2,1)} %param.19) | data formatting | bytes 19660800 | tf_op args[4]
  246.5 3.0 convolution_convert_fusion
  249.6 1.3 copy.87
  250.9 28.2 %fusion.1 = bf16[12,640,640]{1,2,0:T(8,128)(2,1)} fusion(f32[12,640,640]{1,2,0:T(8,128)} %get-tuple-element.143, bf16[1,12,640,640]{2,3,1,0:T(8,128)(2,1)} %copy.88, f32[12,640]{1,0:T(8,128)S(1)} %log_add_fusion, pred[640,640]{0,1:T(8,128)(4,1)S(1)} %broadcast_compare_fusion, bf16[640,12,64]{0,2,1:T(8,128)(2,1)} %bitcast.73, bf16[640,12,64]{0,2,1:T(8,128)(2,1)} %bitcast.68), kind=kOutput, calls=%fused_computation.2 | convolution fusion | flops 1307451520 | bytes 41728000 | tf_op jit(solution)/shard_map/sub | solution.py:164
  279.2 5.8 convert_reduce_fusion.5
  284.9 1.8 copy-done
  287.0 3.2 multiply_convert_fusion.1
  290.2 11.5 %convert_reduce_fusion.4 = (f32[12,64]{1,0:T(8,128)S(1)}, bf16[12,64,640]{2,1,0:T(8,128)(2,1)S(1)}) fusion(bf16[640,12,64]{0,2,1:T(8,128)(2,1)S(1)} %bitcast.74, f32[12,640,640]{1,2,0:T(8,128)} %get-tuple-element.143, f32[12,640]{1,0:T(8,128)S(1)} %log_add_fusion, pred[640,640]{0,1:T(8,128)(4,1)S(1)} %broadcast_compare_fusion), kind=kOutput, calls=%fused_computation.73 | convolution fusion | flops 645364992 | bytes 22070272 | tf_op jit(solution)/shard_map/hqk,qhd->khd/dot_general | solution.py:184
  301.8 0.9 copy-done.30
  302.8 7.9 %convolution_bitcast_fusion = f32[768,2304]{0,1:T(8,128)} fusion(bf16[640,768]{1,0:T(8,128)(2,1)S(1)} %copy-done.29, bf16[640,768]{0,1:T(8,128)(2,1)S(1)} %bitcast.81, bf16[640,768]{0,1:T(8,128)(2,1)S(1)} %bitcast.69, bf16[640,768]{0,1:T(8,128)(2,1)S(1)} %bitcast.65), kind=kOutput, calls=%fused_computation.41 | convolution fusion | flops 2273771520 | bytes 11010048 | tf_op jit(solution)/shard_map/td,tc->dc/dot_general | solution.py:194
  310.7 8.2 %copy.92 = f32[768,2304]{1,0:T(8,128)} copy(f32[768,2304]{0,1:T(8,128)} %convolution_bitcast_fusion) | data formatting | bytes 14155776 | tf_op jit(solution)/shard_map/td,tc->dc/dot_general | solution.py:194
  318.9 6.6 %fusion.75 = f32[768,3072]{1,0:T(8,128)S(1)} fusion(bf16[640,3072]{1,0:T(8,128)(2,1)} %copy-done.9, f32[640,768]{1,0:T(8,128)S(1)} %get-tuple-element.145, f32[768]{0:T(1024)S(1)} %get-tuple-element.111, f32[768]{0:T(1024)S(1)} %get-tuple-element.112, f32[640]{0:T(1024)S(1)} %add_rsqrt_fusion.1, f32[640]{0:T(1024)S(1)} %broadcast_multiply_fusion.7), kind=kOutput, calls=%fused_computation.145 | convolution fusion | flops 3022356480 | bytes 15346688 | tf_op jit(solution)/shard_map/td,tf->df/dot_general | solution.py:139
  325.5 6.0 pad_maximum_fusion
  332.5 13.9 %copy.94 = bf16[1,12,640,640]{3,2,1,0:T(8,128)(2,1)} copy(bf16[1,12,640,640]{2,3,1,0:T(8,128)(2,1)} %bitcast.60) | data formatting | bytes 19660800
  346.4 39.7 %all-reduce = f32[12,768]{1,0:T(8,128)S(1)} all-reduce(f32[12,768]{1,0:T(8,128)S(1)} %concatenate.15), channel_id=4, replica_groups=mesh['dp'=4,'fsdp'=8] {'dp','fsdp'}, use_global_device_ids=true, to_apply=%region_24.25.clone | all-reduce | flops 9216 | bytes 73728
  386.2 0.7 multiply_reduce_fusion.8
  386.9 6.0 add_convert_fusion.1
  392.9 1.7 multiply_reduce_fusion.7
  394.6 180.7 %reduce-scatter.4.cloned.1.call-done = f32[24,5376]{1,0:T(8,128)} async-done(((f32[768,5376]{1,0:T(8,128)}), f32[24,5376]{1,0:T(8,128)}) %reduce-scatter.4.cloned.1.call-update) | async-done | bytes 516112 | tf_op jit(solution)/shard_map/reduce_scatter | solution.py:274
  575.4 1.8 multiply_reduce_fusion.6
  579.2 13.9 %copy.93 = bf16[1,12,640,640]{3,2,1,0:T(8,128)(2,1)} copy(bf16[1,12,640,640]{2,3,1,0:T(8,128)(2,1)} %get-tuple-element.137) | data formatting | bytes 19660800
  593.2 39.3 %psum.7 = f32[]{:T(128)} all-reduce(f32[]{:T(128)S(6)} %add.235), channel_id=1, replica_groups=mesh['dp'=4,'fsdp'=8] {'dp','fsdp'}, use_global_device_ids=true, to_apply=%region_26.27 | all-reduce | flops 1 | bytes 8 | tf_op jit(solution)/shard_map/psum | solution.py:283
  633.3 1.4 fusion.78
  634.7 1.2 fusion.80
  636.0 1.5 fusion.82
  (111 shorter events, 4.4 us)
Async XLA Ops:
  7.2 90.8 %all-gather.4.cloned.1.call-start = ((), (), s32[]{:S(2)}) async-start(), calls=%async_computation.2 | async-start | bytes 8515584 | tf_op jit(solution)/shard_map/all_gather | solution.py:256
  9.0 152.9 %all-gather.6.cloned.1.call-start = ((), (), s32[]{:S(2)}) async-start(), calls=%async_computation.3 | async-start | bytes 6082560 | tf_op jit(solution)/shard_map/all_gather | solution.py:257
  10.8 382.1 %reduce-scatter.6.cloned.1.call-start = ((), (), s32[]{:S(2)}) async-start(), calls=%async_computation.5 | async-start | bytes 12165120 | tf_op jit(solution)/shard_map/reduce_scatter | solution.py:275
  83.5 14.0 %copy-start.27 = (s32[1,640]{1,0:T(1,128)S(1)}, s32[1,640]{1,0:T(1,128)}, u32[]{:S(2)}) copy-start(s32[1,640]{1,0:T(1,128)} %param.17) | copy-start | bytes 7684
  83.5 14.4 %copy-start.28 = (bf16[640,768]{1,0:T(8,128)(2,1)S(1)}, bf16[640,768]{1,0:T(8,128)(2,1)}, u32[]{:S(2)}) copy-start(bf16[640,768]{1,0:T(8,128)(2,1)} %param.15) | copy-start | bytes 2949124
  104.5 14.5 %copy-start.4 = (bf16[640,768]{0,1:T(8,128)(2,1)}, bf16[640,768]{0,1:T(8,128)(2,1)S(1)}, u32[]{:S(2)}) copy-start(bf16[640,768]{0,1:T(8,128)(2,1)S(1)} %copy.83) | copy-start | bytes 2949124
  105.2 13.9 %copy-start.2 = (bf16[640,768]{0,1:T(8,128)(2,1)}, bf16[640,768]{0,1:T(8,128)(2,1)S(1)}, u32[]{:S(2)}) copy-start(bf16[640,768]{0,1:T(8,128)(2,1)S(1)} %copy.84) | copy-start | bytes 2949124
  107.1 29.7 %copy-start.16 = (bf16[640,768]{0,1:T(8,128)(2,1)}, bf16[640,768]{0,1:T(8,128)(2,1)S(1)}, u32[]{:S(2)}) copy-start(bf16[640,768]{0,1:T(8,128)(2,1)S(1)} %copy.82) | copy-start | bytes 2949124
  161.9 27.4 %slice-start.2 = ((s8[5898240]{0:T(1024)(128)(4,1)}), s8[4194304]{0:T(1024)(128)(4,1)S(1)}, s32[]{:S(2)}) async-start(s8[5898240]{0:T(1024)(128)(4,1)} %bitcast.79), calls=%async_computation.8 | async-start | bytes 8388608
  165.4 23.9 %slice-start.3 = ((s8[5898240]{0:T(1024)(128)(4,1)}), s8[1703936]{0:T(1024)(128)(4,1)S(1)}, s32[]{:S(2)}) async-start(s8[5898240]{0:T(1024)(128)(4,1)} %bitcast.79), calls=%async_computation.9 | async-start | bytes 3407872
  189.3 3.8 copy-start.8
  195.9 17.3 %slice-start = ((s8[8257536]{0:T(1024)(128)(4,1)}), s8[4194304]{0:T(1024)(128)(4,1)S(1)}, s32[]{:S(2)}) async-start(s8[8257536]{0:T(1024)(128)(4,1)} %bitcast.77), calls=%async_computation.6 | async-start | bytes 8388608
  202.3 10.9 %slice-start.1 = ((s8[8257536]{0:T(1024)(128)(4,1)}), s8[4063232]{0:T(1024)(128)(4,1)S(1)}, s32[]{:S(2)}) async-start(s8[8257536]{0:T(1024)(128)(4,1)} %bitcast.77), calls=%async_computation.7 | async-start | bytes 8126464
  213.2 3.8 copy-start.9
  213.2 5.8 copy-start.18
  217.7 1.3 copy-start.6
  231.0 344.4 %reduce-scatter.4.cloned.1.call-start = ((), (), s32[]{:S(2)}) async-start(), calls=%async_computation.4 | async-start | bytes 17031168 | tf_op jit(solution)/shard_map/reduce_scatter | solution.py:274
  250.9 28.3 %copy-start.3 = (bf16[640,768]{0,1:T(8,128)(2,1)S(1)}, bf16[640,768]{0,1:T(8,128)(2,1)}, u32[]{:S(2)}) copy-start(bf16[640,768]{0,1:T(8,128)(2,1)} %copy-done.2) | copy-start | bytes 2949124
  279.2 7.6 %copy-start = (bf16[12,640,640]{1,2,0:T(8,128)(2,1)S(1)}, bf16[12,640,640]{1,2,0:T(8,128)(2,1)}, u32[]{:S(2)}) copy-start(bf16[12,640,640]{1,2,0:T(8,128)(2,1)} %fusion.1) | copy-start | bytes 29491204
  279.2 7.8 %copy-start.5 = (bf16[640,768]{0,1:T(8,128)(2,1)S(1)}, bf16[640,768]{0,1:T(8,128)(2,1)}, u32[]{:S(2)}) copy-start(bf16[640,768]{0,1:T(8,128)(2,1)} %copy-done.4) | copy-start | bytes 2949124
  287.0 14.8 %copy-start.10 = (bf16[12,64,640]{2,1,0:T(8,128)(2,1)}, bf16[12,64,640]{2,1,0:T(8,128)(2,1)S(1)}, u32[]{:S(2)}) copy-start(bf16[12,64,640]{2,1,0:T(8,128)(2,1)S(1)} %get-tuple-element.151) | copy-start | bytes 2949124
  287.0 3.2 copy-start.19
  290.2 11.6 %copy-start.17 = (bf16[12,64,640]{2,1,0:T(8,128)(2,1)}, bf16[12,64,640]{2,1,0:T(8,128)(2,1)S(1)}, u32[]{:S(2)}) copy-start(bf16[12,64,640]{2,1,0:T(8,128)(2,1)S(1)} %multiply_convert_fusion.1) | copy-start | bytes 2949124
  290.2 12.5 %copy-start.29 = (bf16[640,768]{1,0:T(8,128)(2,1)S(1)}, bf16[640,768]{1,0:T(8,128)(2,1)}, u32[]{:S(2)}) copy-start(bf16[640,768]{1,0:T(8,128)(2,1)} %param.15) | copy-start | bytes 2949124
  301.8 1.0 copy-start.30
  318.8 6.6 %copy-start.1 = (f32[768,2304]{1,0:T(8,128)S(1)}, f32[768,2304]{1,0:T(8,128)}, u32[]{:S(2)}) copy-start(f32[768,2304]{1,0:T(8,128)} %copy.92) | copy-start | bytes 21233668
  332.4 54.4 %copy-start.7 = (f32[640,768]{1,0:T(8,128)S(1)}, f32[640,768]{1,0:T(8,128)}, u32[]{:S(2)}) copy-start(f32[640,768]{1,0:T(8,128)} %copy-done.6) | copy-start | bytes 5898244
  332.5 54.4 %copy-start.11 = (bf16[12,64,640]{2,1,0:T(8,128)(2,1)S(1)}, bf16[12,64,640]{2,1,0:T(8,128)(2,1)}, u32[]{:S(2)}) copy-start(bf16[12,64,640]{2,1,0:T(8,128)(2,1)} %copy-done.10) | copy-start | bytes 2949124
  386.2 6.7 %copy-start.24 = (f32[12,768]{1,0:T(8,128)}, f32[12,768]{1,0:T(8,128)S(1)}, u32[]{:S(2)}) copy-start(f32[12,768]{1,0:T(8,128)S(1)} %all-reduce) | copy-start | bytes 110596
  579.1 54.1 %copy-start.25 = (f32[12,24]{1,0:T(8,128)S(1)}, f32[12,24]{1,0:T(8,128)}, u32[]{:S(2)}) copy-start(f32[12,24]{1,0:T(8,128)} %param.22) | copy-start | bytes 3460
  579.1 54.1 %copy-start.26 = (f32[12,24]{1,0:T(8,128)S(1)}, f32[12,24]{1,0:T(8,128)}, u32[]{:S(2)}) copy-start(f32[12,24]{1,0:T(8,128)} %param.28) | copy-start | bytes 3460
  579.1 55.6 %copy-start.14 = (f32[120,768]{1,0:T(8,128)S(1)}, f32[120,768]{1,0:T(8,128)}, u32[]{:S(2)}) copy-start(f32[120,768]{1,0:T(8,128)} %param.21) | copy-start | bytes 1105924
  579.1 55.6 %copy-start.15 = (f32[120,768]{1,0:T(8,128)S(1)}, f32[120,768]{1,0:T(8,128)}, u32[]{:S(2)}) copy-start(f32[120,768]{1,0:T(8,128)} %reduce-scatter.6.cloned.1.call-done) | copy-start | bytes 1105924
  579.2 55.6 %copy-start.22 = (f32[120,768]{1,0:T(8,128)S(1)}, f32[120,768]{1,0:T(8,128)}, u32[]{:S(2)}) copy-start(f32[120,768]{1,0:T(8,128)} %param.27) | copy-start | bytes 1105924
  579.2 55.5 %copy-start.23 = (f32[120,768]{1,0:T(8,128)S(1)}, f32[120,768]{1,0:T(8,128)}, u32[]{:S(2)}) copy-start(f32[120,768]{1,0:T(8,128)} %param.24) | copy-start | bytes 1105924
  579.2 56.8 %copy-start.12 = (f32[24,5376]{1,0:T(8,128)S(1)}, f32[24,5376]{1,0:T(8,128)}, u32[]{:S(2)}) copy-start(f32[24,5376]{1,0:T(8,128)} %param.20) | copy-start | bytes 1548292
  579.2 56.8 %copy-start.13 = (f32[24,5376]{1,0:T(8,128)S(1)}, f32[24,5376]{1,0:T(8,128)}, u32[]{:S(2)}) copy-start(f32[24,5376]{1,0:T(8,128)} %reduce-scatter.4.cloned.1.call-done) | copy-start | bytes 1548292
  579.2 56.8 %copy-start.20 = (f32[24,5376]{1,0:T(8,128)S(1)}, f32[24,5376]{1,0:T(8,128)}, u32[]{:S(2)}) copy-start(f32[24,5376]{1,0:T(8,128)} %param.26) | copy-start | bytes 1548292
  579.2 56.8 %copy-start.21 = (f32[24,5376]{1,0:T(8,128)S(1)}, f32[24,5376]{1,0:T(8,128)}, u32[]{:S(2)}) copy-start(f32[24,5376]{1,0:T(8,128)} %param.23) | copy-start | bytes 1548292
Sparse Core Ops, SparseCore 0:
  11.6 80.3 all-gather.3
  95.5 66.3 all-gather.5
  231.2 146.7 reduce-scatter.5
  385.2 190.0 reduce-scatter.3
where the time goes:
time: 656 us; the launch traced here: 646 us
  waiting for transfers between devices  195 us (30%)
  matrix products  154 us (23%)
  blocking collectives  151 us (23%)
  local copies, waits for them, and re-layouts  75.2 us (11%)
  other arithmetic  51.4 us (8%)
  between operations  19.3 us (3%)
    reduce_scatter x1, waiting for transfers between devices, body(): lax.psum_scatter(full_in, ('dp', 'fsdp'), scatter_dimension=0, tiled=True)  181 us
    all_gather x1, blocking collectives, body(): lax.all_gather(low_small, ('dp', 'fsdp'), axis=1, tiled=True)  71.6 us
    unnamed x74, local copies, waits for them, and re-layouts  61.7 us
    unnamed x1, blocking collectives  39.7 us
    psum x1, blocking collectives, body(): total_squares = lax.psum(local_squares, ('dp', 'fsdp'))  39.3 us
    sub x1, matrix products, backward(): grad_probs - jnp.sum(attn_probs * grad_probs, axis=2, keepdims=True)  28.2 us
    dot_general x1, matrix products, forward(): jnp.dot(hidden_low, weight_in[:, 3 * model_width:], preferred_element_typ...  23.9 us
    broadcast_in_dim x1, other arithmetic, body(): scores.astype(jnp.bfloat16)[None]  17.7 us
  transfers between devices with their start and end apart: 4, of which 2 were waited for; matrix products, arithmetic and copies ran while one was open for 29% of the time, Pallas kernels for 0%

commit v1 on v0

--- a/solution.py
+++ b/solution.py
@@ -280,7 +280,7 @@
         + jnp.sum(owned_out * owned_out)
         + jnp.sum(owned_small * owned_small)
     )
-    total_squares = lax.psum(local_squares, ("dp", "fsdp"))
+    total_squares = lax.psum(lax.psum(local_squares, "fsdp"), "dp")
     grad_norm = jnp.sqrt(total_squares)
     threshold = clip_scale * math.sqrt(PARAMS)
     factor = jnp.minimum(1.0, threshold / (grad_norm + 1e-06))

time: 656 us -> 657 us (level)
  waiting for transfers between devices: 195 us -> 209 us
  blocking collectives: 151 us -> 139 us
    reduce_scatter x1, waiting for transfers between devices: 181 us -> 194 us  [body(): lax.psum_scatter(full_in, ('dp', 'fsdp'), scatter_dimension=0, tiled=True)]
    psum x1 -> x2, blocking collectives: 39.3 us -> 26.5 us  [body(): total_squares = lax.psum(lax.psum(local_squares, 'fsdp'), 'dp')]
  transfers between devices with their start and end apart: 4 -> 4, of which waited for: 2 -> 2; matrix products, arithmetic and copies ran while one was open for 29% -> 27% of each run, Pallas kernels for 0% -> 0%
where the time goes in v1:
time: 657 us; the launch traced here: 647 us
  waiting for transfers between devices  209 us (32%)
  matrix products  154 us (23%)
  blocking collectives  139 us (21%)
  local copies, waits for them, and re-layouts  75.1 us (11%)
  other arithmetic  51.3 us (8%)
  between operations  19.4 us (3%)
    reduce_scatter x1, waiting for transfers between devices, body(): lax.psum_scatter(full_in, ('dp', 'fsdp'), scatter_dimension=0, tiled=True)  194 us
    all_gather x1, blocking collectives, body(): lax.all_gather(low_small, ('dp', 'fsdp'), axis=1, tiled=True)  71.6 us
    unnamed x74, local copies, waits for them, and re-layouts  61.6 us
    unnamed x1, blocking collectives  40.6 us
    sub x1, matrix products, backward(): grad_probs - jnp.sum(attn_probs * grad_probs, axis=2, keepdims=True)  28.2 us
    psum x2, blocking collectives, body(): total_squares = lax.psum(lax.psum(local_squares, 'fsdp'), 'dp')  26.5 us
    dot_general x1, matrix products, forward(): jnp.dot(hidden_low, weight_in[:, 3 * model_width:], preferred_element_typ...  23.9 us
    broadcast_in_dim x1, other arithmetic, body(): scores.astype(jnp.bfloat16)[None]  17.7 us
  transfers between devices with their start and end apart: 4, of which 2 were waited for; matrix products, arithmetic and copies ran while one was open for 27% of the time, Pallas kernels for 0%

profile of v1, /device:TPU:0, one launch (start us, length us, event | category | flops | bytes accessed | tf_op | source)
XLA Modules:
  0.0 647.3 jit_solution(1729423751871745051)
XLA Ops:
  7.2 1.8 convert_element_type.143
  9.1 1.7 convert_element_type.154
  10.8 0.7 convert_bitcast_fusion.1
  11.5 71.6 %all-gather = bf16[32,24,12]{1,2,0:T(8,128)(2,1)S(1)} all-gather(bf16[1,24,12]{1,2,0:T(8,128)(2,1)S(1)} %convert_bitcast_fusion.1), channel_id=1, replica_groups=mesh['dp'=4,'fsdp'=8] {'dp','fsdp'}, dimensions={0}, use_global_device_ids=true | all-gather | bytes 19008 | tf_op jit(solution)/shard_map/all_gather | solution.py:258
  83.5 14.0 %copy.85 = bf16[1,12,640,640]{2,3,1,0:T(8,128)(2,1)} copy(bf16[1,12,640,640]{3,2,1,0:T(8,128)(2,1)} %param.16) | data formatting | bytes 19660800 | tf_op args[1]
  98.0 4.5 fusion.34
  102.6 1.3 fusion.45
  105.2 1.9 copy.82
  107.1 11.9 %select_reduce_fusion = (f32[12,640]{1,0:T(8,128)S(1)}, f32[12,640,640]{1,2,0:T(8,128)}) fusion(pred[640,640]{0,1:T(8,128)(4,1)S(1)} %broadcast_compare_fusion, bf16[1,12,640,640]{2,3,1,0:T(8,128)(2,1)} %copy.85, bf16[640,12,64]{0,2,1:T(8,128)(2,1)S(1)} %bitcast.63, bf16[640,12,64]{0,2,1:T(8,128)(2,1)S(1)} %bitcast.61), kind=kOutput, calls=%fused_computation.11 | convolution fusion | flops 653713920 | bytes 31897600 | tf_op jit(solution)/shard_map/qhd,khd->hqk/dot_general | solution.py:54
  119.0 17.7 %convert_bitcast_fusion = (bf16[1,12,640,640]{2,3,1,0:T(8,128)(2,1)}, f32[12,640]{1,0:T(8,128)S(1)}) fusion(f32[12,640,640]{1,2,0:T(8,128)} %get-tuple-element.143, f32[12,640]{1,0:T(8,128)S(1)} %get-tuple-element.142, pred[640,640]{0,1:T(8,128)(4,1)S(1)} %broadcast_compare_fusion), kind=kLoop, calls=%fused_computation.18 | loop fusion | flops 19653120 | bytes 29962240 | tf_op jit(solution)/shard_map/broadcast_in_dim | solution.py:299
  136.8 10.8 %fusion.55 = bf16[12,64,640]{2,1,0:T(8,128)(2,1)} fusion(bf16[640,12,64]{0,2,1:T(8,128)(2,1)S(1)} %bitcast.67, f32[12,640,640]{1,2,0:T(8,128)} %get-tuple-element.143, f32[12,640]{1,0:T(8,128)S(1)} %get-tuple-element.138, f32[12,640]{1,0:T(8,128)S(1)} %get-tuple-element.142, pred[640,640]{0,1:T(8,128)(4,1)S(1)} %broadcast_compare_fusion), kind=kOutput, calls=%fused_computation.92 | convolution fusion | flops 649297920 | bytes 22097920 | tf_op jit(solution)/shard_map/hqk,khd->qhd/dot_general | solution.py:66
  147.6 14.3 %all-gather.6.cloned.1.call-done = bf16[3840,768]{1,0:T(8,128)(2,1)} async-done(((bf16[120,768]{1,0:T(8,128)(2,1)}), bf16[3840,768]{1,0:T(8,128)(2,1)}) %all-gather.6.cloned.1.call-update) | async-done | bytes 5898256 | tf_op jit(solution)/shard_map/all_gather | solution.py:257
  161.9 3.1 fusion.86
  165.4 23.9 %multiply_convert_fusion = (bf16[640,3072]{1,0:T(8,128)(2,1)S(1)}, f32[640,3072]{1,0:T(8,128)}, f32[640,3072]{1,0:T(8,128)}) fusion(f32[3072]{0:T(1024)S(1)} %add.221, bf16[768,5376]{1,0:T(8,128)(2,1)} %all-gather.4.cloned.1.call-done, f32[640,768]{1,0:T(8,128)S(1)} %get-tuple-element.145, f32[768]{0:T(1024)S(1)} %get-tuple-element.111, ...), kind=kOutput, calls=%fused_computation.27 | convolution fusion | flops 3152117760 | bytes 26369024 | tf_op jit(solution)/shard_map/dot_general | solution.py:79
  189.3 3.4 fusion.87
  193.2 1.0 fusion.44
  194.2 1.8 convert_reduce_fusion.2
  195.9 6.4 fusion.69
  202.3 10.9 %convert_reduce_fusion = (f32[3072]{0:T(1024)S(1)}, bf16[640,3072]{1,0:T(8,128)(2,1)S(1)}) fusion(f32[640,3072]{1,0:T(8,128)} %get-tuple-element.136, bf16[3840,768]{1,0:T(8,128)(2,1)} %all-gather.6.cloned.1.call-done, f32[640,768]{1,0:T(8,128)S(1)} %get-tuple-element.132, f32[640,3072]{1,0:T(8,128)} %get-tuple-element.146, f32[3072]{0:T(1024)S(1)} %add.221), kind=kOutput, calls=%fused_computation.25 | convolution fusion | flops 3053810688 | bytes 26370048 | tf_op jit(solution)/shard_map/td,fd->tf/dot_general | solution.py:133
  213.3 3.8 multiply_reduce_fusion.1
  217.7 1.3 copy-done.6
  219.0 2.5 fusion.66
  221.5 9.5 %pad_maximum_fusion.1 = f32[3840,768]{1,0:T(8,128)} fusion(f32[3072,768]{1,0:T(8,128)} %fusion.69, f32[768,768]{1,0:T(8,128)} %fusion.66), kind=kLoop, calls=%fused_computation.13 | loop fusion | flops 2949120 | bytes 23592960 | tf_op jit(solution)/shard_map/concatenate | solution.py:216
  231.1 15.4 %copy.88 = bf16[1,12,640,640]{2,3,1,0:T(8,128)(2,1)} copy(bf16[1,12,640,640]{3,2,1,0:T(8,128)(2,1)} %param.19) | data formatting | bytes 19660800 | tf_op args[4]
  246.5 3.0 convolution_convert_fusion
  249.6 1.3 copy.87
  250.9 28.2 %fusion.1 = bf16[12,640,640]{1,2,0:T(8,128)(2,1)} fusion(f32[12,640,640]{1,2,0:T(8,128)} %get-tuple-element.143, bf16[1,12,640,640]{2,3,1,0:T(8,128)(2,1)} %copy.88, f32[12,640]{1,0:T(8,128)S(1)} %log_add_fusion, pred[640,640]{0,1:T(8,128)(4,1)S(1)} %broadcast_compare_fusion, bf16[640,12,64]{0,2,1:T(8,128)(2,1)} %bitcast.73, bf16[640,12,64]{0,2,1:T(8,128)(2,1)} %bitcast.68), kind=kOutput, calls=%fused_computation.2 | convolution fusion | flops 1307451520 | bytes 41728000 | tf_op jit(solution)/shard_map/sub | solution.py:164
  279.2 5.8 convert_reduce_fusion.5
  284.9 1.8 copy-done
  287.0 3.2 multiply_convert_fusion.1
  290.2 11.5 %convert_reduce_fusion.4 = (f32[12,64]{1,0:T(8,128)S(1)}, bf16[12,64,640]{2,1,0:T(8,128)(2,1)S(1)}) fusion(bf16[640,12,64]{0,2,1:T(8,128)(2,1)S(1)} %bitcast.74, f32[12,640,640]{1,2,0:T(8,128)} %get-tuple-element.143, f32[12,640]{1,0:T(8,128)S(1)} %log_add_fusion, pred[640,640]{0,1:T(8,128)(4,1)S(1)} %broadcast_compare_fusion), kind=kOutput, calls=%fused_computation.73 | convolution fusion | flops 645364992 | bytes 22070272 | tf_op jit(solution)/shard_map/hqk,qhd->khd/dot_general | solution.py:184
  301.8 0.9 copy-done.30
  302.8 7.9 %convolution_bitcast_fusion = f32[768,2304]{0,1:T(8,128)} fusion(bf16[640,768]{1,0:T(8,128)(2,1)S(1)} %copy-done.29, bf16[640,768]{0,1:T(8,128)(2,1)S(1)} %bitcast.81, bf16[640,768]{0,1:T(8,128)(2,1)S(1)} %bitcast.69, bf16[640,768]{0,1:T(8,128)(2,1)S(1)} %bitcast.65), kind=kOutput, calls=%fused_computation.41 | convolution fusion | flops 2273771520 | bytes 11010048 | tf_op jit(solution)/shard_map/td,tc->dc/dot_general | solution.py:194
  310.7 8.2 %copy.92 = f32[768,2304]{1,0:T(8,128)} copy(f32[768,2304]{0,1:T(8,128)} %convolution_bitcast_fusion) | data formatting | bytes 14155776 | tf_op jit(solution)/shard_map/td,tc->dc/dot_general | solution.py:194
  318.9 6.6 %fusion.75 = f32[768,3072]{1,0:T(8,128)S(1)} fusion(bf16[640,3072]{1,0:T(8,128)(2,1)} %copy-done.9, f32[640,768]{1,0:T(8,128)S(1)} %get-tuple-element.145, f32[768]{0:T(1024)S(1)} %get-tuple-element.111, f32[768]{0:T(1024)S(1)} %get-tuple-element.112, f32[640]{0:T(1024)S(1)} %add_rsqrt_fusion.1, f32[640]{0:T(1024)S(1)} %broadcast_multiply_fusion.7), kind=kOutput, calls=%fused_computation.145 | convolution fusion | flops 3022356480 | bytes 15346688 | tf_op jit(solution)/shard_map/td,tf->df/dot_general | solution.py:139
  325.5 6.0 pad_maximum_fusion
  332.7 40.6 %all-reduce = f32[12,768]{1,0:T(8,128)S(1)} all-reduce(f32[12,768]{1,0:T(8,128)S(1)} %concatenate.15), channel_id=4, replica_groups=mesh['dp'=4,'fsdp'=8] {'dp','fsdp'}, use_global_device_ids=true, to_apply=%region_24.25.clone | all-reduce | flops 9216 | bytes 73728
  374.0 6.1 add_convert_fusion.1
  380.1 1.7 multiply_reduce_fusion.7
  381.8 194.5 %reduce-scatter.4.cloned.1.call-done = f32[24,5376]{1,0:T(8,128)} async-done(((f32[768,5376]{1,0:T(8,128)}), f32[24,5376]{1,0:T(8,128)}) %reduce-scatter.4.cloned.1.call-update) | async-done | bytes 516112 | tf_op jit(solution)/shard_map/reduce_scatter | solution.py:274
  576.3 1.8 multiply_reduce_fusion.6
  580.0 13.8 %copy.94 = bf16[1,12,640,640]{3,2,1,0:T(8,128)(2,1)} copy(bf16[1,12,640,640]{2,3,1,0:T(8,128)(2,1)} %bitcast.60) | data formatting | bytes 19660800
  593.8 20.2 %psum.14 = f32[]{:T(128)} all-reduce(f32[]{:T(128)S(6)} %add.237), channel_id=1, replica_groups=mesh['dp'=4,'fsdp'=8] {'fsdp'}, use_global_device_ids=true, to_apply=%region_26.27 | all-reduce | flops 1 | bytes 8 | tf_op jit(solution)/shard_map/psum | solution.py:283
  614.0 13.9 %copy.93 = bf16[1,12,640,640]{3,2,1,0:T(8,128)(2,1)} copy(bf16[1,12,640,640]{2,3,1,0:T(8,128)(2,1)} %get-tuple-element.137) | data formatting | bytes 19660800
  628.0 6.3 psum.15
  635.0 1.4 fusion.78
  636.5 1.2 fusion.80
  637.7 1.5 fusion.82
  (112 shorter events, 5.1 us)
Async XLA Ops:
  7.2 90.8 %all-gather.4.cloned.1.call-start = ((), (), s32[]{:S(2)}) async-start(), calls=%async_computation.2 | async-start | bytes 8515584 | tf_op jit(solution)/shard_map/all_gather | solution.py:256
  9.0 152.9 %all-gather.6.cloned.1.call-start = ((), (), s32[]{:S(2)}) async-start(), calls=%async_computation.3 | async-start | bytes 6082560 | tf_op jit(solution)/shard_map/all_gather | solution.py:257
  10.8 369.3 %reduce-scatter.6.cloned.1.call-start = ((), (), s32[]{:S(2)}) async-start(), calls=%async_computation.5 | async-start | bytes 12165120 | tf_op jit(solution)/shard_map/reduce_scatter | solution.py:275
  83.5 14.0 %copy-start.27 = (s32[1,640]{1,0:T(1,128)S(1)}, s32[1,640]{1,0:T(1,128)}, u32[]{:S(2)}) copy-start(s32[1,640]{1,0:T(1,128)} %param.17) | copy-start | bytes 7684
  83.5 14.4 %copy-start.28 = (bf16[640,768]{1,0:T(8,128)(2,1)S(1)}, bf16[640,768]{1,0:T(8,128)(2,1)}, u32[]{:S(2)}) copy-start(bf16[640,768]{1,0:T(8,128)(2,1)} %param.15) | copy-start | bytes 2949124
  104.5 14.5 %copy-start.4 = (bf16[640,768]{0,1:T(8,128)(2,1)}, bf16[640,768]{0,1:T(8,128)(2,1)S(1)}, u32[]{:S(2)}) copy-start(bf16[640,768]{0,1:T(8,128)(2,1)S(1)} %copy.83) | copy-start | bytes 2949124
  105.2 13.9 %copy-start.2 = (bf16[640,768]{0,1:T(8,128)(2,1)}, bf16[640,768]{0,1:T(8,128)(2,1)S(1)}, u32[]{:S(2)}) copy-start(bf16[640,768]{0,1:T(8,128)(2,1)S(1)} %copy.84) | copy-start | bytes 2949124
  107.1 29.7 %copy-start.16 = (bf16[640,768]{0,1:T(8,128)(2,1)}, bf16[640,768]{0,1:T(8,128)(2,1)S(1)}, u32[]{:S(2)}) copy-start(bf16[640,768]{0,1:T(8,128)(2,1)S(1)} %copy.82) | copy-start | bytes 2949124
  161.9 27.4 %slice-start.2 = ((s8[5898240]{0:T(1024)(128)(4,1)}), s8[4194304]{0:T(1024)(128)(4,1)S(1)}, s32[]{:S(2)}) async-start(s8[5898240]{0:T(1024)(128)(4,1)} %bitcast.79), calls=%async_computation.8 | async-start | bytes 8388608
  165.4 23.9 %slice-start.3 = ((s8[5898240]{0:T(1024)(128)(4,1)}), s8[1703936]{0:T(1024)(128)(4,1)S(1)}, s32[]{:S(2)}) async-start(s8[5898240]{0:T(1024)(128)(4,1)} %bitcast.79), calls=%async_computation.9 | async-start | bytes 3407872
  189.3 3.8 copy-start.8
  195.9 17.3 %slice-start = ((s8[8257536]{0:T(1024)(128)(4,1)}), s8[4194304]{0:T(1024)(128)(4,1)S(1)}, s32[]{:S(2)}) async-start(s8[8257536]{0:T(1024)(128)(4,1)} %bitcast.77), calls=%async_computation.6 | async-start | bytes 8388608
  202.3 10.9 %slice-start.1 = ((s8[8257536]{0:T(1024)(128)(4,1)}), s8[4063232]{0:T(1024)(128)(4,1)S(1)}, s32[]{:S(2)}) async-start(s8[8257536]{0:T(1024)(128)(4,1)} %bitcast.77), calls=%async_computation.7 | async-start | bytes 8126464
  213.2 3.8 copy-start.9
  213.2 5.8 copy-start.18
  217.7 1.3 copy-start.6
  231.0 345.2 %reduce-scatter.4.cloned.1.call-start = ((), (), s32[]{:S(2)}) async-start(), calls=%async_computation.4 | async-start | bytes 17031168 | tf_op jit(solution)/shard_map/reduce_scatter | solution.py:274
  250.9 28.3 %copy-start.3 = (bf16[640,768]{0,1:T(8,128)(2,1)S(1)}, bf16[640,768]{0,1:T(8,128)(2,1)}, u32[]{:S(2)}) copy-start(bf16[640,768]{0,1:T(8,128)(2,1)} %copy-done.2) | copy-start | bytes 2949124
  279.2 7.6 %copy-start = (bf16[12,640,640]{1,2,0:T(8,128)(2,1)S(1)}, bf16[12,640,640]{1,2,0:T(8,128)(2,1)}, u32[]{:S(2)}) copy-start(bf16[12,640,640]{1,2,0:T(8,128)(2,1)} %fusion.1) | copy-start | bytes 29491204
  279.2 7.8 %copy-start.5 = (bf16[640,768]{0,1:T(8,128)(2,1)S(1)}, bf16[640,768]{0,1:T(8,128)(2,1)}, u32[]{:S(2)}) copy-start(bf16[640,768]{0,1:T(8,128)(2,1)} %copy-done.4) | copy-start | bytes 2949124
  287.0 14.8 %copy-start.10 = (bf16[12,64,640]{2,1,0:T(8,128)(2,1)}, bf16[12,64,640]{2,1,0:T(8,128)(2,1)S(1)}, u32[]{:S(2)}) copy-start(bf16[12,64,640]{2,1,0:T(8,128)(2,1)S(1)} %get-tuple-element.151) | copy-start | bytes 2949124
  287.0 3.2 copy-start.19
  290.2 11.6 %copy-start.17 = (bf16[12,64,640]{2,1,0:T(8,128)(2,1)}, bf16[12,64,640]{2,1,0:T(8,128)(2,1)S(1)}, u32[]{:S(2)}) copy-start(bf16[12,64,640]{2,1,0:T(8,128)(2,1)S(1)} %multiply_convert_fusion.1) | copy-start | bytes 2949124
  290.2 12.5 %copy-start.29 = (bf16[640,768]{1,0:T(8,128)(2,1)S(1)}, bf16[640,768]{1,0:T(8,128)(2,1)}, u32[]{:S(2)}) copy-start(bf16[640,768]{1,0:T(8,128)(2,1)} %param.15) | copy-start | bytes 2949124
  301.8 1.0 copy-start.30
  318.8 6.6 %copy-start.1 = (f32[768,2304]{1,0:T(8,128)S(1)}, f32[768,2304]{1,0:T(8,128)}, u32[]{:S(2)}) copy-start(f32[768,2304]{1,0:T(8,128)} %copy.92) | copy-start | bytes 21233668
  331.5 42.5 %copy-start.7 = (f32[640,768]{1,0:T(8,128)S(1)}, f32[640,768]{1,0:T(8,128)}, u32[]{:S(2)}) copy-start(f32[640,768]{1,0:T(8,128)} %copy-done.6) | copy-start | bytes 5898244
  331.5 42.5 %copy-start.11 = (bf16[12,64,640]{2,1,0:T(8,128)(2,1)S(1)}, bf16[12,64,640]{2,1,0:T(8,128)(2,1)}, u32[]{:S(2)}) copy-start(bf16[12,64,640]{2,1,0:T(8,128)(2,1)} %copy-done.10) | copy-start | bytes 2949124
  373.3 6.8 %copy-start.24 = (f32[12,768]{1,0:T(8,128)}, f32[12,768]{1,0:T(8,128)S(1)}, u32[]{:S(2)}) copy-start(f32[12,768]{1,0:T(8,128)S(1)} %all-reduce) | copy-start | bytes 110596
  614.0 21.0 %copy-start.25 = (f32[12,24]{1,0:T(8,128)S(1)}, f32[12,24]{1,0:T(8,128)}, u32[]{:S(2)}) copy-start(f32[12,24]{1,0:T(8,128)} %param.22) | copy-start | bytes 3460
  614.0 21.0 %copy-start.26 = (f32[12,24]{1,0:T(8,128)S(1)}, f32[12,24]{1,0:T(8,128)}, u32[]{:S(2)}) copy-start(f32[12,24]{1,0:T(8,128)} %param.28) | copy-start | bytes 3460
  614.0 22.5 %copy-start.14 = (f32[120,768]{1,0:T(8,128)S(1)}, f32[120,768]{1,0:T(8,128)}, u32[]{:S(2)}) copy-start(f32[120,768]{1,0:T(8,128)} %param.21) | copy-start | bytes 1105924
  614.0 22.5 %copy-start.15 = (f32[120,768]{1,0:T(8,128)S(1)}, f32[120,768]{1,0:T(8,128)}, u32[]{:S(2)}) copy-start(f32[120,768]{1,0:T(8,128)} %reduce-scatter.6.cloned.1.call-done) | copy-start | bytes 1105924
  614.0 22.5 %copy-start.22 = (f32[120,768]{1,0:T(8,128)S(1)}, f32[120,768]{1,0:T(8,128)}, u32[]{:S(2)}) copy-start(f32[120,768]{1,0:T(8,128)} %param.27) | copy-start | bytes 1105924
  614.0 22.5 %copy-start.23 = (f32[120,768]{1,0:T(8,128)S(1)}, f32[120,768]{1,0:T(8,128)}, u32[]{:S(2)}) copy-start(f32[120,768]{1,0:T(8,128)} %param.24) | copy-start | bytes 1105924
  614.0 23.7 %copy-start.12 = (f32[24,5376]{1,0:T(8,128)S(1)}, f32[24,5376]{1,0:T(8,128)}, u32[]{:S(2)}) copy-start(f32[24,5376]{1,0:T(8,128)} %param.20) | copy-start | bytes 1548292
  614.0 23.7 %copy-start.13 = (f32[24,5376]{1,0:T(8,128)S(1)}, f32[24,5376]{1,0:T(8,128)}, u32[]{:S(2)}) copy-start(f32[24,5376]{1,0:T(8,128)} %reduce-scatter.4.cloned.1.call-done) | copy-start | bytes 1548292
  614.0 23.7 %copy-start.20 = (f32[24,5376]{1,0:T(8,128)S(1)}, f32[24,5376]{1,0:T(8,128)}, u32[]{:S(2)}) copy-start(f32[24,5376]{1,0:T(8,128)} %param.26) | copy-start | bytes 1548292
  614.0 23.7 %copy-start.21 = (f32[24,5376]{1,0:T(8,128)S(1)}, f32[24,5376]{1,0:T(8,128)}, u32[]{:S(2)}) copy-start(f32[24,5376]{1,0:T(8,128)} %param.23) | copy-start | bytes 1548292
Sparse Core Ops, SparseCore 0:
  11.6 80.3 all-gather.3
  95.5 66.3 all-gather.5
  231.2 148.0 reduce-scatter.5
  386.6 189.6 reduce-scatter.3
